TPU v7x, 128 devices: a whole 4x4x4 slice. The times are simulated.
128 devices in a mesh: gx: 16 (over x, y), gy: 8 (over z, core).
Axes of the slice: x: 4, y: 4, z: 4, core: 2. Of those that a mesh axis runs over, the one named last changes fastest.
Arguments:
- head: float32 [512, 384, 128], P('gx', 'gy'), may hold values from -6 to 6
- conductivity: float32 [512, 384, 128], P('gx', 'gy'), may hold values from 0.1 to 10
- storage: float32 [512, 384, 128], P('gx', 'gy'), may hold values from 0.3 to 3
- recharge: float32 [512, 384, 128], P('gx', 'gy'), may hold values from -6 to 6
- misfit: float32 [512, 384, 128], P('gx', 'gy'), may hold values from -6 to 6
- reservoir_cell: int32 [2048], P(('gx', 'gy')), may hold values from 0 to 196607
- pumping: float32 [2048], P(('gx', 'gy')), may hold values from -25 to 25
- observed: float32 [2048], P(('gx', 'gy')), may hold values from -25 to 25
- tile_owner: int32 [12288, 1], P(('gx', 'gy')), may hold values from 0 to 127; in each aligned block of 96 rows (0 to 95, 96 to 191, ...) at most 2 rows name the same one
- tile_inverse: bfloat16 [32768, 128, 128], P(('gx', 'gy')), may hold values from -0.01 to 0.05
- zone_of_column: int32 [512, 384], P('gx', 'gy'), may hold values from 0 to 49151
Outputs:
- new_head: float32 [512, 384, 128], P('gx', 'gy')
- zone_gradient: float32 [49152], P(('gx', 'gy'))
Inputs may be any that keep to these rules, and one draw needn't show every extreme that they name: `tile_owner`: in each device's block of 96 tiles no owner is named by more than 2 tiles. `reservoir_cell`: A flat index into the 32 x 48 x 128 block of the device that holds the reservoir.
All inputs are finite; a program needn't handle non-finite values.
Results may differ from a plain program's by a relative error of at most 0.0016.
Values may be sent and summed in bfloat16 or wider, within the bound.
A program may use at most 128 MiB of HBM per device.

v0:
```python
import jax
import jax.numpy as jnp
from jax import lax
from jax.sharding import PartitionSpec as P

AGG = 4
CYCLES = 2
SWEEPS = 2
ZONES_DEV = 384


relax = 0.8


def extended(value, sides, width):
    for axis, dim in sides:
        count, length = (lax.axis_size(axis), value.shape[dim])
        up = [(i, (i + 1) % count) for i in range(count - 1)]
        down = [(j, i) for i, j in up]
        last = lax.slice_in_dim(value, length - width, length, axis=dim)
        initial = lax.slice_in_dim(value, 0, width, axis=dim)
        before = lax.ppermute(last, axis, up)
        after = lax.ppermute(initial, axis, down)
        value = jnp.concatenate([before, value, after], axis=dim)
    return value


def neighbours(padded):
    center = padded[..., 1:-1, 1:-1, :]
    zero = jnp.zeros_like(center[..., :1])
    above = jnp.concatenate([center[..., 1:], zero], axis=-1)
    below = jnp.concatenate([zero, center[..., :-1]], axis=-1)
    return (
        center,
        [
            padded[..., 2:, 1:-1, :],
            padded[..., :-2, 1:-1, :],
            padded[..., 1:-1, 2:, :],
            padded[..., 1:-1, :-2, :],
            above,
            below,
        ],
    )


def conductances(padded_k):
    center, beside_all = neighbours(padded_k)
    return [0.5 * (center + other) for other in beside_all]


def apply_operator(padded, diag_part, conds):
    center, beside_all = neighbours(padded)
    result = diag_part * center
    for face, other in zip(conds, beside_all):
        result = result + face * (center - other)
    return result


def row_total(diag_part, conds):
    total = diag_part
    for face in conds:
        total = total + face
    return total


def face_gradient(padded_head, padded_adjoint):
    head_c, head_n = neighbours(padded_head)
    adj_c, adj_n = neighbours(padded_adjoint)
    grad = jnp.zeros_like(head_c)
    for head_o, adj_o in zip(head_n, adj_n):
        grad = grad - 0.5 * (adj_c - adj_o) * (head_c - head_o)
    return grad


def rim(state):
    return extended(state, (("gx", 1), ("gy", 2)), 1)


def on_device(
    head,
    conductivity,
    storage,
    recharge,
    misfit,
    reservoir_cell,
    pumping,
    observed,
    tile_owner,
    tile_inverse,
    zone_of_column,
):
    rows_x, rows_y, layers = head.shape
    count_x = lax.axis_size("gx")
    count_y = lax.axis_size("gy")
    devices = count_x * count_y
    capacity = tile_inverse.shape[0] // devices
    tiles_x = rows_x // AGG
    tiles_y = rows_y // AGG

    def place(values):
        field = jnp.zeros((rows_x * rows_y * layers,), jnp.float32).at[reservoir_cell].add(values)
        return field.reshape(rows_x, rows_y, layers)

    coeff_stack = jnp.stack([conductivity, storage, head])
    padded = extended(coeff_stack, (("gx", 1), ("gy", 2)), 1)
    conds = conductances(padded[0])
    applied = apply_operator(padded[2], storage, conds)
    total = row_total(storage, conds)
    rhs = jnp.stack([recharge + place(pumping) - applied, misfit + place(observed)])

    def smooth(state):
        for step in range(SWEEPS):
            if state is None:
                state = relax * rhs / total
            else:
                near = extended(state, (("gx", 1), ("gy", 2)), 1)
                state = state + relax * (rhs - apply_operator(near, storage, conds)) / total
        return state

    owners = tile_owner[:, 0]
    order = jnp.arange(owners.shape[0], dtype=jnp.int32)
    same = owners[:, None] == owners[None, :]
    earlier = order[:, None] > order[None, :]
    rank = jnp.sum(same & earlier, axis=1)
    slot = owners * capacity + rank
    state = None
    for cycle in range(CYCLES):
        state = smooth(state)
        sums = (
            (rhs - apply_operator(rim(state), storage, conds))
            .reshape(2, tiles_x, AGG, tiles_y, AGG, layers)
            .sum(axis=(2, 4))
        )
        tile_rows = (
            jnp.transpose(sums, (1, 2, 0, 3))
            .reshape(tiles_x * tiles_y, 2, layers)
            .astype(jnp.bfloat16)
        )
        outgoing = jnp.zeros((devices * capacity, 2, layers), jnp.bfloat16).at[slot].set(tile_rows)
        product = jnp.einsum(
            "smij,smfj->smfi",
            tile_inverse.reshape(devices, capacity, layers, layers),
            lax.all_to_all(
                outgoing.reshape(devices, capacity, 2, layers),
                ("gx", "gy"),
                split_axis=0,
                concat_axis=0,
                tiled=True,
            ),
            preferred_element_type=jnp.float32,
        )
        returned = lax.all_to_all(product, ("gx", "gy"), split_axis=0, concat_axis=0, tiled=True)
        own_rows = returned.reshape(devices * capacity, 2, layers)[slot]
        spread = jnp.transpose(own_rows.reshape(tiles_x, tiles_y, 2, layers), (2, 0, 1, 3))
        state = state + jnp.repeat(jnp.repeat(spread, AGG, axis=1), AGG, axis=2)
        state = smooth(state)
    new_head = head + state[0]
    final_rim = rim(jnp.stack([new_head, state[1]]))
    grad = face_gradient(final_rim[0], final_rim[1])
    column = jnp.sum(grad, axis=-1) / layers
    zone_total = devices * ZONES_DEV
    local_zones = jax.ops.segment_sum(
        column.reshape(-1), zone_of_column.reshape(-1), num_segments=zone_total
    )
    zone_gradient = lax.psum_scatter(local_zones, ("gx", "gy"), scatter_dimension=0, tiled=True)
    return (new_head, zone_gradient)


def solution(mesh):
    placed = (
        P("gx", "gy", None),
        P("gx", "gy", None),
        P("gx", "gy", None),
        P("gx", "gy", None),
        P("gx", "gy", None),
        P(("gx", "gy")),
        P(("gx", "gy")),
        P(("gx", "gy")),
        P(("gx", "gy"), None),
        P(("gx", "gy"), None, None),
        P("gx", "gy"),
    )
    return jax.shard_map(
        on_device,
        mesh=mesh,
        in_specs=placed,
        out_specs=(P("gx", "gy", None), P(("gx", "gy"))),
        check_vma=False,
    )
```

profile of v0, /device:TPU:1, one launch (start us, length us, event | category | flops | bytes accessed | tf_op | source)
XLA Modules:
  0.0 498.1 jit_solution(14746278285362628272)
XLA Ops:
  8.2 4.0 collective-permute-start
  14.6 2.8 collective-permute-done.1
  17.4 5.5 %collective-permute-start.2 = (f32[3,34,1,128]{3,2,1,0:T(1,128)S(1)}, f32[3,34,1,128]{3,2,1,0:T(1,128)S(1)}, u32[]{:S(2)}, u32[]{:S(2)}) collective-permute-start(f32[3,34,1,128]{3,2,1,0:T(1,128)S(1)} %get-tuple-element.11), channel_id=1, source_target_pairs={{0,1},{1,2},{2,3},{3,4},{4,5},{5,6},{6,7},{8,9},{9,10},{10,11},{11... | collective-permute-start | bytes 156680 | tf_op jit(solution)/shard_map/ppermute | solution.py:22
  34.5 4.0 collective-permute-start.5
  41.6 4.2 collective-permute-start.7
  46.9 2.6 fusion.146
  50.8 4.7 collective-permute-start.9
  58.6 5.1 %collective-permute-start.11 = (f32[2,34,1,128]{3,2,1,0:T(1,128)S(1)}, f32[2,34,1,128]{3,2,1,0:T(1,128)S(1)}, u32[]{:S(2)}, u32[]{:S(2)}) collective-permute-start(f32[2,34,1,128]{3,2,1,0:T(1,128)S(1)} %get-tuple-element.34), channel_id=1, source_target_pairs={{0,1},{1,2},{2,3},{3,4},{4,5},{5,6},{6,7},{8,9},{9,10},{10,11},{11... | collective-permute-start | bytes 104456 | tf_op jit(solution)/shard_map/ppermute | solution.py:22
  64.8 4.0 fusion.128
  70.7 3.5 scatter_fusion
  74.2 26.7 %all_to_all.20 = bf16[128,2,2,128]{3,2,1,0:T(2,128)(2,1)S(1)} all-to-all(bf16[128,2,2,128]{3,2,1,0:T(2,128)(2,1)S(1)} %bitcast.81), channel_id=1, replica_groups=mesh['gx'=16,'gy'=8] {'gx','gy'}, dimensions={0} | all-to-all | bytes 262144 | tf_op jit(solution)/shard_map/all_to_all | solution.py:143
  100.9 8.5 %fusion.223 = f32[128,2,2,128]{3,2,1,0:T(2,128)} fusion(bf16[128,2,2,128]{3,2,1,0:T(2,128)(2,1)S(1)} %all_to_all.20, bf16[128,2,128,128]{3,2,1,0:T(8,128)(2,1)} %bitcast.61), kind=kOutput, calls=%fused_computation.381 | convolution fusion | flops 16777216 | bytes 8781824 | tf_op jit(solution)/shard_map/smij,smfj->smfi/dot_general | solution.py:140
  109.4 4.5 all-to-all-start.1
  114.2 10.6 %all-to-all-done.1 = f32[128,2,2,128]{3,2,1,0:T(2,128)S(1)} async-done(((f32[128,2,2,128]{3,2,1,0:T(2,128)}), f32[128,2,2,128]{3,2,1,0:T(2,128)S(1)}, u32[]{:S(2)}, u32[]{:S(2)}) %all-to-all-start.1) | async-done | bytes 262176 | tf_op jit(solution)/shard_map/all_to_all | solution.py:152
  128.4 4.0 collective-permute-start.13
  133.6 4.2 collective-permute-start.14
  141.3 2.6 fusion.113
  145.3 4.6 collective-permute-start.17
  151.1 2.9 collective-permute-start.18
  154.0 3.9 collective-permute-start.19
  158.9 2.6 fusion.95
  162.9 4.6 collective-permute-start.21
  170.6 5.1 %collective-permute-start.23 = (f32[2,34,1,128]{3,2,1,0:T(1,128)S(1)}, f32[2,34,1,128]{3,2,1,0:T(1,128)S(1)}, u32[]{:S(2)}, u32[]{:S(2)}) collective-permute-start(f32[2,34,1,128]{3,2,1,0:T(1,128)S(1)} %get-tuple-element.28), channel_id=1, source_target_pairs={{0,1},{1,2},{2,3},{3,4},{4,5},{5,6},{6,7},{8,9},{9,10},{10,11},{11... | collective-permute-start | bytes 104456 | tf_op jit(solution)/shard_map/ppermute | solution.py:22
  176.7 2.6 fusion.77
  180.7 4.6 collective-permute-start.25
  188.4 5.1 %collective-permute-start.27 = (f32[2,34,1,128]{3,2,1,0:T(1,128)S(1)}, f32[2,34,1,128]{3,2,1,0:T(1,128)S(1)}, u32[]{:S(2)}, u32[]{:S(2)}) collective-permute-start(f32[2,34,1,128]{3,2,1,0:T(1,128)S(1)} %get-tuple-element.26), channel_id=1, source_target_pairs={{0,1},{1,2},{2,3},{3,4},{4,5},{5,6},{6,7},{8,9},{9,10},{10,11},{11... | collective-permute-start | bytes 104456 | tf_op jit(solution)/shard_map/ppermute | solution.py:22
  194.5 2.6 fusion.59
  198.5 4.6 collective-permute-start.29
  206.2 5.1 %collective-permute-start.31 = (f32[2,34,1,128]{3,2,1,0:T(1,128)S(1)}, f32[2,34,1,128]{3,2,1,0:T(1,128)S(1)}, u32[]{:S(2)}, u32[]{:S(2)}) collective-permute-start(f32[2,34,1,128]{3,2,1,0:T(1,128)S(1)} %get-tuple-element.24), channel_id=1, source_target_pairs={{0,1},{1,2},{2,3},{3,4},{4,5},{5,6},{6,7},{8,9},{9,10},{10,11},{11... | collective-permute-start | bytes 104456 | tf_op jit(solution)/shard_map/ppermute | solution.py:22
  212.3 3.9 fusion.41
  218.2 3.5 scatter_fusion.1
  221.6 27.7 %all_to_all.21 = bf16[128,2,2,128]{3,2,1,0:T(2,128)(2,1)S(1)} all-to-all(bf16[128,2,2,128]{3,2,1,0:T(2,128)(2,1)S(1)} %bitcast.80), channel_id=1, replica_groups=mesh['gx'=16,'gy'=8] {'gx','gy'}, dimensions={0} | all-to-all | bytes 262144 | tf_op jit(solution)/shard_map/all_to_all | solution.py:143
  249.3 7.8 %fusion.224 = f32[128,2,2,128]{3,2,1,0:T(2,128)S(1)} fusion(bf16[128,2,2,128]{3,2,1,0:T(2,128)(2,1)S(1)} %all_to_all.21, bf16[128,2,128,128]{3,2,1,0:T(8,128)(2,1)} %bitcast.62), kind=kOutput, calls=%fused_computation.382 | convolution fusion | flops 16777216 | bytes 8781824 | tf_op jit(solution)/shard_map/smij,smfj->smfi/dot_general | solution.py:140
  257.1 15.2 %all_to_all.22 = f32[128,2,2,128]{3,2,1,0:T(2,128)S(1)} all-to-all(f32[128,2,2,128]{3,2,1,0:T(2,128)S(1)} %fusion.224), channel_id=1, replica_groups=mesh['gx'=16,'gy'=8] {'gx','gy'}, dimensions={0} | all-to-all | bytes 524288 | tf_op jit(solution)/shard_map/all_to_all | solution.py:152
  276.0 4.0 collective-permute-start.33
  281.2 4.1 collective-permute-start.34
  285.4 2.2 collective-permute-start.35
  288.8 2.6 fusion.26
  292.8 4.6 collective-permute-start.37
  298.6 2.9 collective-permute-start.38
  301.5 3.9 collective-permute-start.39
  306.4 2.6 fusion.8
  309.3 4.1 collective-permute-start.40
  314.7 3.8 collective-permute-done.41
  318.5 5.4 %collective-permute-start.42 = (f32[2,34,1,128]{3,2,1,0:T(1,128)S(1)}, f32[2,34,1,128]{3,2,1,0:T(1,128)S(1)}, u32[]{:S(2)}, u32[]{:S(2)}) collective-permute-start(f32[2,34,1,128]{3,2,1,0:T(1,128)S(1)} %get-tuple-element.17), channel_id=1, source_target_pairs={{0,1},{1,2},{2,3},{3,4},{4,5},{5,6},{6,7},{8,9},{9,10},{10,11},{11... | collective-permute-start | bytes 104456 | tf_op jit(solution)/shard_map/ppermute | solution.py:22
  325.9 3.2 collective-permute-done.43
  331.9 9.2 %scatter_custom_fusion.4 = f32[49152]{0:T(1024)} fusion(s32[1536]{0:T(1024)S(1)} %reshape.133, f32[1536]{0:T(1024)S(1)} %reshape.135, f32[]{:T(128)} %constant.9.clone.1), kind=kCustom, calls=%fused_computation.305 | custom fusion | flops 1536 | bytes 196612 | tf_op jit(solution)/shard_map/scatter-add | solution.py:162
  341.2 148.7 %all-reduce.29.cloned.1.call-done = f32[49152]{0:T(1024)} async-done(((f32[49152]{0:T(1024)}), f32[49152]{0:T(1024)}) %all-reduce.29.cloned.1.call-update) | async-done | bytes 196624
  (198 shorter events, 73.4 us)
Async XLA Ops:
  8.2 6.4 %collective-permute-start = (f32[3,1,48,128]{3,2,1,0:T(8,128)S(1)}, f32[3,1,48,128]{3,2,1,0:T(8,128)S(1)}, u32[]{:S(2)}, u32[]{:S(2)}) collective-permute-start(f32[3,1,48,128]{3,2,1,0:T(8,128)S(1)} %get-tuple-element.13), channel_id=1, source_target_pairs={{0,8},{8,16},{16,24},{24,32},{32,40},{40,48},{48,56},{56,64},{64,7... | collective-permute-start | bytes 221192 | tf_op jit(solution)/shard_map/ppermute | solution.py:22
  12.2 5.1 %collective-permute-start.1 = (f32[3,1,48,128]{3,2,1,0:T(8,128)S(1)}, f32[3,1,48,128]{3,2,1,0:T(8,128)S(1)}, u32[]{:S(2)}, u32[]{:S(2)}) collective-permute-start(f32[3,1,48,128]{3,2,1,0:T(8,128)S(1)} %get-tuple-element.14), channel_id=1, source_target_pairs={{8,0},{16,8},{24,16},{32,24},{40,32},{48,40},{56,48},{64,56},{72,6... | collective-permute-start | bytes 221192 | tf_op jit(solution)/shard_map/ppermute | solution.py:23
  17.4 10.1 %collective-permute-start.2 = (f32[3,34,1,128]{3,2,1,0:T(1,128)S(1)}, f32[3,34,1,128]{3,2,1,0:T(1,128)S(1)}, u32[]{:S(2)}, u32[]{:S(2)}) collective-permute-start(f32[3,34,1,128]{3,2,1,0:T(1,128)S(1)} %get-tuple-element.11), channel_id=1, source_target_pairs={{0,1},{1,2},{2,3},{3,4},{4,5},{5,6},{6,7},{8,9},{9,10},{10,11},{11... | collective-permute-start | bytes 156680 | tf_op jit(solution)/shard_map/ppermute | solution.py:22
  23.0 5.4 %collective-permute-start.3 = (f32[3,34,1,128]{3,2,1,0:T(1,128)S(1)}, f32[3,34,1,128]{3,2,1,0:T(1,128)S(1)}, u32[]{:S(2)}, u32[]{:S(2)}) collective-permute-start(f32[3,34,1,128]{3,2,1,0:T(1,128)S(1)} %get-tuple-element.12), channel_id=1, source_target_pairs={{1,0},{2,1},{3,2},{4,3},{5,4},{6,5},{7,6},{9,8},{10,9},{11,10},{12... | collective-permute-start | bytes 156680 | tf_op jit(solution)/shard_map/ppermute | solution.py:23
  31.3 33.5 %copy-start.1 = (f32[32,48,128]{2,1,0:T(8,128)}, f32[32,48,128]{2,1,0:T(8,128)S(1)}, u32[]{:S(2)}) copy-start(f32[32,48,128]{2,1,0:T(8,128)S(1)} %get-tuple-element.6) | copy-start | bytes 2359300
  31.3 33.5 %copy-start.4 = (f32[32,48,128]{2,1,0:T(8,128)}, f32[32,48,128]{2,1,0:T(8,128)S(1)}, u32[]{:S(2)}) copy-start(f32[32,48,128]{2,1,0:T(8,128)S(1)} %get-tuple-element.7) | copy-start | bytes 2359300
  33.2 5.5 %collective-permute-start.4 = (f32[2,1,48,128]{3,2,1,0:T(8,128)S(1)}, f32[2,1,48,128]{3,2,1,0:T(8,128)S(1)}, u32[]{:S(2)}, u32[]{:S(2)}) collective-permute-start(f32[2,1,48,128]{3,2,1,0:T(8,128)S(1)} %get-tuple-element.74), channel_id=1, source_target_pairs={{8,0},{16,8},{24,16},{32,24},{40,32},{48,40},{56,48},{64,56},{72,6... | collective-permute-start | bytes 147464 | tf_op jit(solution)/shard_map/ppermute | solution.py:23
  34.5 5.2 %collective-permute-start.5 = (f32[2,1,48,128]{3,2,1,0:T(8,128)S(1)}, f32[2,1,48,128]{3,2,1,0:T(8,128)S(1)}, u32[]{:S(2)}, u32[]{:S(2)}) collective-permute-start(f32[2,1,48,128]{3,2,1,0:T(8,128)S(1)} %get-tuple-element.73), channel_id=1, source_target_pairs={{0,8},{8,16},{16,24},{24,32},{32,40},{40,48},{48,56},{56,64},{64,7... | collective-permute-start | bytes 147464 | tf_op jit(solution)/shard_map/ppermute | solution.py:22
  39.7 6.7 %collective-permute-start.6 = (f32[2,34,1,128]{3,2,1,0:T(1,128)S(1)}, f32[2,34,1,128]{3,2,1,0:T(1,128)S(1)}, u32[]{:S(2)}, u32[]{:S(2)}) collective-permute-start(f32[2,34,1,128]{3,2,1,0:T(1,128)S(1)} %get-tuple-element.35), channel_id=1, source_target_pairs={{1,0},{2,1},{3,2},{4,3},{5,4},{6,5},{7,6},{9,8},{10,9},{11,10},{12... | collective-permute-start | bytes 104456 | tf_op jit(solution)/shard_map/ppermute | solution.py:23
  41.6 5.2 %collective-permute-start.7 = (f32[2,34,1,128]{3,2,1,0:T(1,128)S(1)}, f32[2,34,1,128]{3,2,1,0:T(1,128)S(1)}, u32[]{:S(2)}, u32[]{:S(2)}) collective-permute-start(f32[2,34,1,128]{3,2,1,0:T(1,128)S(1)} %get-tuple-element.36), channel_id=1, source_target_pairs={{0,1},{1,2},{2,3},{3,4},{4,5},{5,6},{6,7},{8,9},{9,10},{10,11},{11... | collective-permute-start | bytes 104456 | tf_op jit(solution)/shard_map/ppermute | solution.py:22
  49.5 6.1 %collective-permute-start.8 = (f32[2,1,48,128]{3,2,1,0:T(8,128)S(1)}, f32[2,1,48,128]{3,2,1,0:T(8,128)S(1)}, u32[]{:S(2)}, u32[]{:S(2)}) collective-permute-start(f32[2,1,48,128]{3,2,1,0:T(8,128)S(1)} %get-tuple-element.70), channel_id=1, source_target_pairs={{8,0},{16,8},{24,16},{32,24},{40,32},{48,40},{56,48},{64,56},{72,6... | collective-permute-start | bytes 147464 | tf_op jit(solution)/shard_map/ppermute | solution.py:23
  50.8 5.9 %collective-permute-start.9 = (f32[2,1,48,128]{3,2,1,0:T(8,128)S(1)}, f32[2,1,48,128]{3,2,1,0:T(8,128)S(1)}, u32[]{:S(2)}, u32[]{:S(2)}) collective-permute-start(f32[2,1,48,128]{3,2,1,0:T(8,128)S(1)} %get-tuple-element.69), channel_id=1, source_target_pairs={{0,8},{8,16},{16,24},{24,32},{32,40},{40,48},{48,56},{56,64},{64,7... | collective-permute-start | bytes 147464 | tf_op jit(solution)/shard_map/ppermute | solution.py:22
  56.7 7.5 %collective-permute-start.10 = (f32[2,34,1,128]{3,2,1,0:T(1,128)S(1)}, f32[2,34,1,128]{3,2,1,0:T(1,128)S(1)}, u32[]{:S(2)}, u32[]{:S(2)}) collective-permute-start(f32[2,34,1,128]{3,2,1,0:T(1,128)S(1)} %get-tuple-element.33), channel_id=1, source_target_pairs={{1,0},{2,1},{3,2},{4,3},{5,4},{6,5},{7,6},{9,8},{10,9},{11,10},{12... | collective-permute-start | bytes 104456 | tf_op jit(solution)/shard_map/ppermute | solution.py:23
  58.6 6.1 %collective-permute-start.11 = (f32[2,34,1,128]{3,2,1,0:T(1,128)S(1)}, f32[2,34,1,128]{3,2,1,0:T(1,128)S(1)}, u32[]{:S(2)}, u32[]{:S(2)}) collective-permute-start(f32[2,34,1,128]{3,2,1,0:T(1,128)S(1)} %get-tuple-element.34), channel_id=1, source_target_pairs={{0,1},{1,2},{2,3},{3,4},{4,5},{5,6},{6,7},{8,9},{9,10},{10,11},{11... | collective-permute-start | bytes 104456 | tf_op jit(solution)/shard_map/ppermute | solution.py:22
  109.4 15.3 %all-to-all-start.1 = ((f32[128,2,2,128]{3,2,1,0:T(2,128)}), f32[128,2,2,128]{3,2,1,0:T(2,128)S(1)}, u32[]{:S(2)}, u32[]{:S(2)}) async-start(f32[128,2,2,128]{3,2,1,0:T(2,128)} %fusion.223), calls=%async_computation.1 | async-start | bytes 524288 | tf_op jit(solution)/shard_map/all_to_all | solution.py:152
  113.9 376.0 %all-reduce.29.cloned.1.call-start = ((), (), s32[]{:S(2)}) async-start(), calls=%async_computation.4 | async-start | bytes 393216
  127.1 5.3 %collective-permute-start.12 = (f32[2,1,48,128]{3,2,1,0:T(8,128)S(1)}, f32[2,1,48,128]{3,2,1,0:T(8,128)S(1)}, u32[]{:S(2)}, u32[]{:S(2)}) collective-permute-start(f32[2,1,48,128]{3,2,1,0:T(8,128)S(1)} %get-tuple-element.66), channel_id=1, source_target_pairs={{8,0},{16,8},{24,16},{32,24},{40,32},{48,40},{56,48},{64,56},{72,6... | collective-permute-start | bytes 147464 | tf_op jit(solution)/shard_map/ppermute | solution.py:23
  128.4 5.2 %collective-permute-start.13 = (f32[2,1,48,128]{3,2,1,0:T(8,128)S(1)}, f32[2,1,48,128]{3,2,1,0:T(8,128)S(1)}, u32[]{:S(2)}, u32[]{:S(2)}) collective-permute-start(f32[2,1,48,128]{3,2,1,0:T(8,128)S(1)} %get-tuple-element.65), channel_id=1, source_target_pairs={{0,8},{8,16},{16,24},{24,32},{32,40},{40,48},{48,56},{56,64},{64,7... | collective-permute-start | bytes 147464 | tf_op jit(solution)/shard_map/ppermute | solution.py:22
  133.6 7.0 %collective-permute-start.14 = (f32[2,34,1,128]{3,2,1,0:T(1,128)S(1)}, f32[2,34,1,128]{3,2,1,0:T(1,128)S(1)}, u32[]{:S(2)}, u32[]{:S(2)}) collective-permute-start(f32[2,34,1,128]{3,2,1,0:T(1,128)S(1)} %get-tuple-element.31), channel_id=1, source_target_pairs={{1,0},{2,1},{3,2},{4,3},{5,4},{6,5},{7,6},{9,8},{10,9},{11,10},{12... | collective-permute-start | bytes 104456 | tf_op jit(solution)/shard_map/ppermute | solution.py:23
  137.9 3.4 collective-permute-start.15
  144.0 5.9 %collective-permute-start.16 = (f32[2,1,48,128]{3,2,1,0:T(8,128)S(1)}, f32[2,1,48,128]{3,2,1,0:T(8,128)S(1)}, u32[]{:S(2)}, u32[]{:S(2)}) collective-permute-start(f32[2,1,48,128]{3,2,1,0:T(8,128)S(1)} %get-tuple-element.62), channel_id=1, source_target_pairs={{8,0},{16,8},{24,16},{32,24},{40,32},{48,40},{56,48},{64,56},{72,6... | collective-permute-start | bytes 147464 | tf_op jit(solution)/shard_map/ppermute | solution.py:23
  145.3 5.8 %collective-permute-start.17 = (f32[2,1,48,128]{3,2,1,0:T(8,128)S(1)}, f32[2,1,48,128]{3,2,1,0:T(8,128)S(1)}, u32[]{:S(2)}, u32[]{:S(2)}) collective-permute-start(f32[2,1,48,128]{3,2,1,0:T(8,128)S(1)} %get-tuple-element.61), channel_id=1, source_target_pairs={{0,8},{8,16},{16,24},{24,32},{32,40},{40,48},{48,56},{56,64},{64,7... | collective-permute-start | bytes 147464 | tf_op jit(solution)/shard_map/ppermute | solution.py:22
  151.1 7.4 %collective-permute-start.18 = (f32[2,34,1,128]{3,2,1,0:T(1,128)S(1)}, f32[2,34,1,128]{3,2,1,0:T(1,128)S(1)}, u32[]{:S(2)}, u32[]{:S(2)}) collective-permute-start(f32[2,34,1,128]{3,2,1,0:T(1,128)S(1)} %get-tuple-element.29), channel_id=1, source_target_pairs={{1,0},{2,1},{3,2},{4,3},{5,4},{6,5},{7,6},{9,8},{10,9},{11,10},{12... | collective-permute-start | bytes 104456 | tf_op jit(solution)/shard_map/ppermute | solution.py:23
  154.0 5.0 collective-permute-start.19
  161.6 5.9 %collective-permute-start.20 = (f32[2,1,48,128]{3,2,1,0:T(8,128)S(1)}, f32[2,1,48,128]{3,2,1,0:T(8,128)S(1)}, u32[]{:S(2)}, u32[]{:S(2)}) collective-permute-start(f32[2,1,48,128]{3,2,1,0:T(8,128)S(1)} %get-tuple-element.58), channel_id=1, source_target_pairs={{8,0},{16,8},{24,16},{32,24},{40,32},{48,40},{56,48},{64,56},{72,6... | collective-permute-start | bytes 147464 | tf_op jit(solution)/shard_map/ppermute | solution.py:23
  162.9 5.8 %collective-permute-start.21 = (f32[2,1,48,128]{3,2,1,0:T(8,128)S(1)}, f32[2,1,48,128]{3,2,1,0:T(8,128)S(1)}, u32[]{:S(2)}, u32[]{:S(2)}) collective-permute-start(f32[2,1,48,128]{3,2,1,0:T(8,128)S(1)} %get-tuple-element.57), channel_id=1, source_target_pairs={{0,8},{8,16},{16,24},{24,32},{32,40},{40,48},{48,56},{56,64},{64,7... | collective-permute-start | bytes 147464 | tf_op jit(solution)/shard_map/ppermute | solution.py:22
  168.7 7.5 %collective-permute-start.22 = (f32[2,34,1,128]{3,2,1,0:T(1,128)S(1)}, f32[2,34,1,128]{3,2,1,0:T(1,128)S(1)}, u32[]{:S(2)}, u32[]{:S(2)}) collective-permute-start(f32[2,34,1,128]{3,2,1,0:T(1,128)S(1)} %get-tuple-element.27), channel_id=1, source_target_pairs={{1,0},{2,1},{3,2},{4,3},{5,4},{6,5},{7,6},{9,8},{10,9},{11,10},{12... | collective-permute-start | bytes 104456 | tf_op jit(solution)/shard_map/ppermute | solution.py:23
  170.6 6.1 %collective-permute-start.23 = (f32[2,34,1,128]{3,2,1,0:T(1,128)S(1)}, f32[2,34,1,128]{3,2,1,0:T(1,128)S(1)}, u32[]{:S(2)}, u32[]{:S(2)}) collective-permute-start(f32[2,34,1,128]{3,2,1,0:T(1,128)S(1)} %get-tuple-element.28), channel_id=1, source_target_pairs={{0,1},{1,2},{2,3},{3,4},{4,5},{5,6},{6,7},{8,9},{9,10},{10,11},{11... | collective-permute-start | bytes 104456 | tf_op jit(solution)/shard_map/ppermute | solution.py:22
  179.4 5.9 %collective-permute-start.24 = (f32[2,1,48,128]{3,2,1,0:T(8,128)S(1)}, f32[2,1,48,128]{3,2,1,0:T(8,128)S(1)}, u32[]{:S(2)}, u32[]{:S(2)}) collective-permute-start(f32[2,1,48,128]{3,2,1,0:T(8,128)S(1)} %get-tuple-element.54), channel_id=1, source_target_pairs={{8,0},{16,8},{24,16},{32,24},{40,32},{48,40},{56,48},{64,56},{72,6... | collective-permute-start | bytes 147464 | tf_op jit(solution)/shard_map/ppermute | solution.py:23
  180.7 5.8 %collective-permute-start.25 = (f32[2,1,48,128]{3,2,1,0:T(8,128)S(1)}, f32[2,1,48,128]{3,2,1,0:T(8,128)S(1)}, u32[]{:S(2)}, u32[]{:S(2)}) collective-permute-start(f32[2,1,48,128]{3,2,1,0:T(8,128)S(1)} %get-tuple-element.53), channel_id=1, source_target_pairs={{0,8},{8,16},{16,24},{24,32},{32,40},{40,48},{48,56},{56,64},{64,7... | collective-permute-start | bytes 147464 | tf_op jit(solution)/shard_map/ppermute | solution.py:22
  186.5 7.5 %collective-permute-start.26 = (f32[2,34,1,128]{3,2,1,0:T(1,128)S(1)}, f32[2,34,1,128]{3,2,1,0:T(1,128)S(1)}, u32[]{:S(2)}, u32[]{:S(2)}) collective-permute-start(f32[2,34,1,128]{3,2,1,0:T(1,128)S(1)} %get-tuple-element.25), channel_id=1, source_target_pairs={{1,0},{2,1},{3,2},{4,3},{5,4},{6,5},{7,6},{9,8},{10,9},{11,10},{12... | collective-permute-start | bytes 104456 | tf_op jit(solution)/shard_map/ppermute | solution.py:23
  188.4 6.1 %collective-permute-start.27 = (f32[2,34,1,128]{3,2,1,0:T(1,128)S(1)}, f32[2,34,1,128]{3,2,1,0:T(1,128)S(1)}, u32[]{:S(2)}, u32[]{:S(2)}) collective-permute-start(f32[2,34,1,128]{3,2,1,0:T(1,128)S(1)} %get-tuple-element.26), channel_id=1, source_target_pairs={{0,1},{1,2},{2,3},{3,4},{4,5},{5,6},{6,7},{8,9},{9,10},{10,11},{11... | collective-permute-start | bytes 104456 | tf_op jit(solution)/shard_map/ppermute | solution.py:22
  197.2 5.9 %collective-permute-start.28 = (f32[2,1,48,128]{3,2,1,0:T(8,128)S(1)}, f32[2,1,48,128]{3,2,1,0:T(8,128)S(1)}, u32[]{:S(2)}, u32[]{:S(2)}) collective-permute-start(f32[2,1,48,128]{3,2,1,0:T(8,128)S(1)} %get-tuple-element.50), channel_id=1, source_target_pairs={{8,0},{16,8},{24,16},{32,24},{40,32},{48,40},{56,48},{64,56},{72,6... | collective-permute-start | bytes 147464 | tf_op jit(solution)/shard_map/ppermute | solution.py:23
  198.5 5.8 %collective-permute-start.29 = (f32[2,1,48,128]{3,2,1,0:T(8,128)S(1)}, f32[2,1,48,128]{3,2,1,0:T(8,128)S(1)}, u32[]{:S(2)}, u32[]{:S(2)}) collective-permute-start(f32[2,1,48,128]{3,2,1,0:T(8,128)S(1)} %get-tuple-element.49), channel_id=1, source_target_pairs={{0,8},{8,16},{16,24},{24,32},{32,40},{40,48},{48,56},{56,64},{64,7... | collective-permute-start | bytes 147464 | tf_op jit(solution)/shard_map/ppermute | solution.py:22
  204.3 7.5 %collective-permute-start.30 = (f32[2,34,1,128]{3,2,1,0:T(1,128)S(1)}, f32[2,34,1,128]{3,2,1,0:T(1,128)S(1)}, u32[]{:S(2)}, u32[]{:S(2)}) collective-permute-start(f32[2,34,1,128]{3,2,1,0:T(1,128)S(1)} %get-tuple-element.23), channel_id=1, source_target_pairs={{1,0},{2,1},{3,2},{4,3},{5,4},{6,5},{7,6},{9,8},{10,9},{11,10},{12... | collective-permute-start | bytes 104456 | tf_op jit(solution)/shard_map/ppermute | solution.py:23
  206.2 6.1 %collective-permute-start.31 = (f32[2,34,1,128]{3,2,1,0:T(1,128)S(1)}, f32[2,34,1,128]{3,2,1,0:T(1,128)S(1)}, u32[]{:S(2)}, u32[]{:S(2)}) collective-permute-start(f32[2,34,1,128]{3,2,1,0:T(1,128)S(1)} %get-tuple-element.24), channel_id=1, source_target_pairs={{0,1},{1,2},{2,3},{3,4},{4,5},{5,6},{6,7},{8,9},{9,10},{10,11},{11... | collective-permute-start | bytes 104456 | tf_op jit(solution)/shard_map/ppermute | solution.py:22
  274.7 5.3 %collective-permute-start.32 = (f32[2,1,48,128]{3,2,1,0:T(8,128)S(1)}, f32[2,1,48,128]{3,2,1,0:T(8,128)S(1)}, u32[]{:S(2)}, u32[]{:S(2)}) collective-permute-start(f32[2,1,48,128]{3,2,1,0:T(8,128)S(1)} %get-tuple-element.46), channel_id=1, source_target_pairs={{8,0},{16,8},{24,16},{32,24},{40,32},{48,40},{56,48},{64,56},{72,6... | collective-permute-start | bytes 147464 | tf_op jit(solution)/shard_map/ppermute | solution.py:23
  276.0 5.2 %collective-permute-start.33 = (f32[2,1,48,128]{3,2,1,0:T(8,128)S(1)}, f32[2,1,48,128]{3,2,1,0:T(8,128)S(1)}, u32[]{:S(2)}, u32[]{:S(2)}) collective-permute-start(f32[2,1,48,128]{3,2,1,0:T(8,128)S(1)} %get-tuple-element.45), channel_id=1, source_target_pairs={{0,8},{8,16},{16,24},{24,32},{32,40},{40,48},{48,56},{56,64},{64,7... | collective-permute-start | bytes 147464 | tf_op jit(solution)/shard_map/ppermute | solution.py:22
  281.2 6.9 %collective-permute-start.34 = (f32[2,34,1,128]{3,2,1,0:T(1,128)S(1)}, f32[2,34,1,128]{3,2,1,0:T(1,128)S(1)}, u32[]{:S(2)}, u32[]{:S(2)}) collective-permute-start(f32[2,34,1,128]{3,2,1,0:T(1,128)S(1)} %get-tuple-element.21), channel_id=1, source_target_pairs={{1,0},{2,1},{3,2},{4,3},{5,4},{6,5},{7,6},{9,8},{10,9},{11,10},{12... | collective-permute-start | bytes 104456 | tf_op jit(solution)/shard_map/ppermute | solution.py:23
  285.4 3.4 collective-permute-start.35
  291.5 5.9 %collective-permute-start.36 = (f32[2,1,48,128]{3,2,1,0:T(8,128)S(1)}, f32[2,1,48,128]{3,2,1,0:T(8,128)S(1)}, u32[]{:S(2)}, u32[]{:S(2)}) collective-permute-start(f32[2,1,48,128]{3,2,1,0:T(8,128)S(1)} %get-tuple-element.42), channel_id=1, source_target_pairs={{8,0},{16,8},{24,16},{32,24},{40,32},{48,40},{56,48},{64,56},{72,6... | collective-permute-start | bytes 147464 | tf_op jit(solution)/shard_map/ppermute | solution.py:23
  292.8 5.8 %collective-permute-start.37 = (f32[2,1,48,128]{3,2,1,0:T(8,128)S(1)}, f32[2,1,48,128]{3,2,1,0:T(8,128)S(1)}, u32[]{:S(2)}, u32[]{:S(2)}) collective-permute-start(f32[2,1,48,128]{3,2,1,0:T(8,128)S(1)} %get-tuple-element.41), channel_id=1, source_target_pairs={{0,8},{8,16},{16,24},{24,32},{32,40},{40,48},{48,56},{56,64},{64,7... | collective-permute-start | bytes 147464 | tf_op jit(solution)/shard_map/ppermute | solution.py:22
  298.6 7.4 %collective-permute-start.38 = (f32[2,34,1,128]{3,2,1,0:T(1,128)S(1)}, f32[2,34,1,128]{3,2,1,0:T(1,128)S(1)}, u32[]{:S(2)}, u32[]{:S(2)}) collective-permute-start(f32[2,34,1,128]{3,2,1,0:T(1,128)S(1)} %get-tuple-element.19), channel_id=1, source_target_pairs={{1,0},{2,1},{3,2},{4,3},{5,4},{6,5},{7,6},{9,8},{10,9},{11,10},{12... | collective-permute-start | bytes 104456 | tf_op jit(solution)/shard_map/ppermute | solution.py:23
  301.5 5.0 collective-permute-start.39
  309.3 5.4 %collective-permute-start.40 = (f32[2,1,48,128]{3,2,1,0:T(8,128)S(1)}, f32[2,1,48,128]{3,2,1,0:T(8,128)S(1)}, u32[]{:S(2)}, u32[]{:S(2)}) collective-permute-start(f32[2,1,48,128]{3,2,1,0:T(8,128)S(1)} %get-tuple-element.37), channel_id=1, source_target_pairs={{0,8},{8,16},{16,24},{24,32},{32,40},{40,48},{48,56},{56,64},{64,7... | collective-permute-start | bytes 147464 | tf_op jit(solution)/shard_map/ppermute | solution.py:22
  313.4 5.1 %collective-permute-start.41 = (f32[2,1,48,128]{3,2,1,0:T(8,128)S(1)}, f32[2,1,48,128]{3,2,1,0:T(8,128)S(1)}, u32[]{:S(2)}, u32[]{:S(2)}) collective-permute-start(f32[2,1,48,128]{3,2,1,0:T(8,128)S(1)} %get-tuple-element.38), channel_id=1, source_target_pairs={{8,0},{16,8},{24,16},{32,24},{40,32},{48,40},{56,48},{64,56},{72,6... | collective-permute-start | bytes 147464 | tf_op jit(solution)/shard_map/ppermute | solution.py:23
  318.5 7.4 %collective-permute-start.42 = (f32[2,34,1,128]{3,2,1,0:T(1,128)S(1)}, f32[2,34,1,128]{3,2,1,0:T(1,128)S(1)}, u32[]{:S(2)}, u32[]{:S(2)}) collective-permute-start(f32[2,34,1,128]{3,2,1,0:T(1,128)S(1)} %get-tuple-element.17), channel_id=1, source_target_pairs={{0,1},{1,2},{2,3},{3,4},{4,5},{5,6},{6,7},{8,9},{9,10},{10,11},{11... | collective-permute-start | bytes 104456 | tf_op jit(solution)/shard_map/ppermute | solution.py:22
  323.9 5.3 %collective-permute-start.43 = (f32[2,34,1,128]{3,2,1,0:T(1,128)S(1)}, f32[2,34,1,128]{3,2,1,0:T(1,128)S(1)}, u32[]{:S(2)}, u32[]{:S(2)}) collective-permute-start(f32[2,34,1,128]{3,2,1,0:T(1,128)S(1)} %get-tuple-element.18), channel_id=1, source_target_pairs={{1,0},{2,1},{3,2},{4,3},{5,4},{6,5},{7,6},{9,8},{10,9},{11,10},{12... | collective-permute-start | bytes 104456 | tf_op jit(solution)/shard_map/ppermute | solution.py:23
  (31 other events, 252.6 us)
Sparse Core Ops, SparseCore 0:
  341.3 148.5 all-reduce.28
where the time goes:
time: 500 us; the launch traced here: 498 us
  waiting for transfers between devices  185 us (37%)
  starting transfers between devices  142 us (28%)
  blocking collectives  69.6 us (14%)
  other arithmetic  48.8 us (10%)
  local copies, waits for them, and re-layouts  21 us (4%)
  matrix products  16.3 us (3%)
  between operations  15.4 us (3%)
    unnamed x2, waiting for transfers between devices  149 us
    ppermute x22, starting transfers between devices, extended(): before = lax.ppermute(last, axis, up)  95.5 us
    all_to_all x2, blocking collectives, on_device(): lax.all_to_all(outgoing.reshape(devices, capacity, 2, layers), ('gx', 'gy...  54.4 us
    ppermute x22, starting transfers between devices, extended(): after = lax.ppermute(initial, axis, down)  41.9 us
    add x7, other arithmetic, smooth(): state = state + relax * (rhs - apply_operator(near, storage, conds)) / total  18.3 us
    dot_general x2, matrix products, on_device(): jnp.einsum('smij,smfj->smfi', tile_inverse.reshape(devices, capacity, lay...  16.3 us
    all_to_all x1, blocking collectives, on_device(): lax.all_to_all(product, ('gx', 'gy'), split_axis=0, concat_axis=0, tiled=...  15.2 us
    ppermute x22, waiting for transfers between devices, extended(): before = lax.ppermute(last, axis, up)  14.9 us
  transfers between devices with their start and end apart: 46, of which 24 were waited for; matrix products, arithmetic and copies ran while one was open for 2% of the time, Pallas kernels for 0%

commit v1 on v0

v1 whole, which is shorter than its diff:
```python
import functools

import jax
import jax.numpy as jnp
from jax import lax
from jax.experimental import pallas as pl
from jax.experimental.pallas import tpu as pltpu
from jax.sharding import PartitionSpec as P

CX, CY, CZ = 32, 48, 128
T = 4
ROWS = CY * 8
PAD = ROWS + 16
TILES = 96
ZDEV = 384
CYCLES = 2
EXCHANGES = 10
RELAX = 0.8
F32, BF16 = jnp.float32, jnp.bfloat16
MESH = pl.DeviceIdType.MESH
CONTRACT_LAST = (((1,), (1,)), ((), ()))


def kernel(
    nx, ny,
    head, cond, stor, rech, misf, cells, pump, obs, owner, mats_in, zone,
    out_head, out_zone,
    nat, mats, kl, hl, kx, hdx, ecf, dg, rs, xs, sx, hx, grad, onat, owner_row, p_out, p_in, zone_hot,
    rbuf, gbuf, cbuf, send_a, recv_a, send_b, recv_b, lz, send_z, recv_z,
    load_sem, mats_sem, out_sem, init_s, init_r, halo_s, halo_r, a_s, a_r, b_s, b_r, z_s, z_r,
):
    n = nx * ny
    me_x, me_y = lax.axis_index("gx"), lax.axis_index("gy")
    me = me_x * ny + me_y
    east, west = (lax.rem(me_x + 1, nx), me_y), (lax.rem(me_x + nx - 1, nx), me_y)
    north, south = (me_x, lax.rem(me_y + 1, ny)), (me_x, lax.rem(me_y + ny - 1, ny))
    in_w, in_e = jnp.where(me_x == 0, 0.0, 1.0), jnp.where(me_x == nx - 1, 0.0, 1.0)
    in_s, in_n = jnp.where(me_y == 0, 0.0, 1.0), jnp.where(me_y == ny - 1, 0.0, 1.0)

    def peer(i):
        other = lax.rem(me + i, n)
        return other, (lax.div(other, ny), lax.rem(other, ny))

    loads = [pltpu.make_async_copy(src, nat.at[i], load_sem.at[i]) for i, src in enumerate((cond, head, stor, rech, misf))]
    for copy in loads:
        copy.start()
    mats_copy = pltpu.make_async_copy(mats_in, mats, mats_sem)
    mats_copy.start()

    barrier = pltpu.get_barrier_semaphore()

    def greet(i, carry):
        pl.semaphore_signal(barrier, inc=1, device_id=peer(i)[1], device_id_type=MESH)
        return carry

    lax.fori_loop(1, n, greet, 0)

    def relayout(i, dst, offset):
        def one(t, carry):
            for s in range(8):
                for block in range(CY // 8):
                    dst[t, pl.ds(offset + block * 64 + s, 8, stride=8), :] = nat[i, 4 * s + t, block * 8:block * 8 + 8, :]
            return carry

        lax.fori_loop(0, T, one, 0)

    loads[0].wait()
    relayout(0, kl, 8)
    loads[1].wait()
    relayout(1, hl, 8)

    pl.semaphore_wait(barrier, n - 1)

    def remote(src, dst, send, recv, device):
        copy = pltpu.make_async_remote_copy(src, dst, send, recv, device_id=device, device_id_type=MESH)
        copy.start()
        return copy

    first = []
    for i, (lay, side) in enumerate(((kl, kx), (hl, hdx))):
        first += [
            remote(nat.at[i, CX - 1], side.at[0], init_s.at[4 * i], init_r.at[4 * i], east),
            remote(nat.at[i, 0], side.at[1], init_s.at[4 * i + 1], init_r.at[4 * i + 1], west),
            remote(lay.at[:, ROWS:ROWS + 8], lay.at[:, 0:8], init_s.at[4 * i + 2], init_r.at[4 * i + 2], north),
            remote(lay.at[:, 8:16], lay.at[:, ROWS + 8:PAD], init_s.at[4 * i + 3], init_r.at[4 * i + 3], south),
        ]

    loads[2].wait()
    relayout(2, dg, 0)
    loads[3].wait()
    relayout(3, rs.at[0], 0)
    loads[4].wait()
    relayout(4, rs.at[1], 0)

    count = cells.shape[1]
    cell = cells[...]
    column = lax.shift_right_logical(cell, 7)
    cell_z = (cell & 127).astype(F32)
    cell_x = jnp.floor((column.astype(F32) + 0.5) * (1.0 / CY)).astype(jnp.int32)
    cell_row = (cell_x & 3) * ROWS + (column - cell_x * CY) * 8 + lax.shift_right_logical(cell_x, 2)
    diag = lax.broadcasted_iota(jnp.int32, (count, count), 0) == lax.broadcasted_iota(jnp.int32, (count, count), 1)

    def upright(row, mask):
        return jnp.sum(jnp.where(mask, jnp.broadcast_to(row, mask.shape), 0.0), axis=1, keepdims=True)

    at_z = lax.broadcasted_iota(jnp.int32, (count, CZ), 1) == upright(cell_z, diag).astype(jnp.int32)
    values = jnp.concatenate([jnp.where(at_z, upright(v[...], diag), 0.0) for v in (pump, obs)], axis=1)
    value_parts = []
    for _ in range(3):
        value_parts.append(values.astype(BF16))
        values = values - value_parts[-1].astype(F32)

    def put_reservoirs(t, carry):
        rows = lax.broadcasted_iota(jnp.int32, (ROWS, count), 0) + t * ROWS
        hot = jnp.where(rows == cell_row, 1.0, 0.0).astype(BF16)
        field = sum(jnp.dot(hot, part, preferred_element_type=F32) for part in value_parts)
        rs[0, t] += field[:, :CZ]
        rs[1, t] += field[:, CZ:]
        return carry

    lax.fori_loop(0, T, put_reservoirs, 0)

    lane = lax.broadcasted_iota(jnp.int32, (128, 128), 1)
    sub = lax.broadcasted_iota(jnp.int32, (128, 128), 0)
    owner_row[...] = -1000.0 - lane[0:1].astype(F32)
    owner_row[0:1, 0:TILES] = owner[...].astype(F32)
    orow = owner_row[...]
    ocol = upright(orow, lane == sub)
    same = ocol == orow
    rank_row = jnp.sum(jnp.where(same & (sub < lane), 1.0, 0.0), axis=0, keepdims=True)
    rank_col = jnp.sum(jnp.where(same & (lane < sub), 1.0, 0.0), axis=1, keepdims=True)
    code_row = orow * 4.0 + rank_row * 2.0
    code_col = ocol * 4.0 + rank_col * 2.0
    down = lax.broadcasted_iota(jnp.int32, (4 * n, 128), 0).astype(F32)
    across = lax.broadcasted_iota(jnp.int32, (128, 4 * n), 1).astype(F32)
    for f in range(2):
        p_out[:, f * 128:f * 128 + 128] = jnp.where(down == code_row + float(f), 1.0, 0.0).astype(BF16)
        p_in[f * 128:f * 128 + 128, :] = jnp.where(across == code_col + float(f), 1.0, 0.0).astype(BF16)
    rbuf[...] = jnp.zeros_like(rbuf)

    zones = zone[...].astype(F32)
    zone_dev = jnp.floor((zones + 0.5) * (1.0 / ZDEV))
    zone_local = zones - zone_dev * ZDEV
    for block in range(T):
        cut = slice(block * ROWS, block * ROWS + ROWS)
        rows = lax.broadcasted_iota(jnp.int32, (ZDEV, ROWS), 0).astype(F32)
        zone_hot[:, cut] = jnp.where(rows == zone_local[:, cut], 1.0, 0.0).astype(BF16)

    for copy in first:
        copy.wait()
    for lay in (kl, hl):
        lay[:, 0:8] = lay[:, 0:8] * in_s
        lay[:, ROWS + 8:PAD] = lay[:, ROWS + 8:PAD] * in_n
    for side in (kx, hdx):
        side[0] = side[0] * in_w
        side[1] = side[1] * in_e

    sub8 = lax.broadcasted_iota(jnp.int32, (8, CZ), 0)
    lane8 = lax.broadcasted_iota(jnp.int32, (8, CZ), 1)
    low_s, high_s, low_z, high_z = sub8 == 0, sub8 == 7, lane8 == 0, lane8 == CZ - 1

    def beside(tile, west_row, east_row, t, y, wrap_z):
        row = pl.multiple_of(y * 8, 8)
        center = tile(t, row + 8)
        if t == 0:
            wst = jnp.where(low_s, jnp.broadcast_to(west_row(y), (8, CZ)), pltpu.roll(tile(T - 1, row + 8), 1, 0))
        else:
            wst = tile(t - 1, row + 8)
        if t == T - 1:
            est = jnp.where(high_s, jnp.broadcast_to(east_row(y), (8, CZ)), pltpu.roll(tile(0, row + 8), 7, 0))
        else:
            est = tile(t + 1, row + 8)
        below, above = pltpu.roll(center, 1, 1), pltpu.roll(center, CZ - 1, 1)
        if not wrap_z:
            below, above = jnp.where(low_z, 0.0, below), jnp.where(high_z, 0.0, above)
        return center, (wst, est, tile(t, row), tile(t, row + 16), below, above)

    def plain(ref):
        return lambda t, row: ref[t, pl.ds(pl.multiple_of(row, 8), 8), :]

    def field_of(p, f):
        return lambda t, row: xs[p, f, t, pl.ds(pl.multiple_of(row, 8), 8), :]

    def side_row(ref, side):
        return lambda y: ref[side, pl.ds(y, 1), :]

    def halo_row(k, side, f):
        return lambda y: hx[k, side, f, pl.ds(y, 1), :]

    def put(p, k, f, t, y, value):
        xs[p, f, t, pl.ds(pl.multiple_of(y * 8 + 8, 8), 8), :] = value
        if t == 0:
            sx[k, 0, f, pl.ds(y, 1), :] = value[0:1]
        if t == T - 1:
            sx[k, 1, f, pl.ds(y, 1), :] = value[7:8]

    def exchange(p, k):
        return [
            remote(sx.at[k, 1], hx.at[k, 0], halo_s.at[k, 0], halo_r.at[k, 0], east),
            remote(sx.at[k, 0], hx.at[k, 1], halo_s.at[k, 1], halo_r.at[k, 1], west),
            remote(xs.at[p, :, :, ROWS:ROWS + 8], xs.at[p, :, :, 0:8], halo_s.at[k, 2], halo_r.at[k, 2], north),
            remote(xs.at[p, :, :, 8:16], xs.at[p, :, :, ROWS + 8:PAD], halo_s.at[k, 3], halo_r.at[k, 3], south),
        ]

    def prepare(y, carry):
        row = pl.multiple_of(y * 8, 8)
        for t in range(T):
            here = (t, pl.ds(row, 8), slice(None))
            k_c, k_all = beside(plain(kl), side_row(kx, 0), side_row(kx, 1), t, y, False)
            h_c, h_all = beside(plain(hl), side_row(hdx, 0), side_row(hdx, 1), t, y, False)
            faces = [0.5 * (k_c + other) for other in k_all]
            storage = dg[here]
            total = storage
            applied = storage * h_c
            for face, other in zip(faces, h_all):
                total = total + face
                applied = applied + face * (h_c - other)
            gain = RELAX / total
            dg[here] = total * (1.0 / RELAX)
            faces[0] = faces[0] if t else jnp.where(low_s, faces[0] * in_w, faces[0])
            faces[1] = faces[1] if t < T - 1 else jnp.where(high_s, faces[1] * in_e, faces[1])
            faces[4] = jnp.where(low_z, 0.0, faces[4])
            faces[5] = jnp.where(high_z, 0.0, faces[5])
            for j in range(6):
                ecf[j, t, pl.ds(row, 8), :] = faces[j] * gain
            for f in range(2):
                rhs = rs[f, t, pl.ds(row, 8), :]
                rhs = (rhs - applied if f == 0 else rhs) * gain
                rs[f, t, pl.ds(row, 8), :] = rhs
                put(0, 0, f, t, y, rhs)
        return carry

    lax.fori_loop(0, CY, prepare, 0)
    ecf[2, :, 0:8] = ecf[2, :, 0:8] * in_s
    ecf[3, :, ROWS - 8:ROWS] = ecf[3, :, ROWS - 8:ROWS] * in_n

    def change(p, k, t, y):
        row = pl.multiple_of(y * 8, 8)
        factors = [ecf[j, t, pl.ds(row, 8), :] for j in range(6)]
        result = []
        for f in range(2):
            center, others = beside(field_of(p, f), halo_row(k, 0, f), halo_row(k, 1, f), t, y, True)
            total = rs[f, t, pl.ds(row, 8), :]
            for factor, other in zip(factors, others):
                total = total + factor * other
            result.append((center, total))
        return result

    def sweep(p, k):
        q = 1 - p

        def one(y, carry):
            for t in range(T):
                for f, (center, total) in enumerate(change(p, k, t, y)):
                    put(q, k + 1, f, t, y, (1.0 - RELAX) * center + total)
            return carry

        lax.fori_loop(0, CY, one, 0)

    def residual(p, k):
        def one(b, carry):
            sums = [jnp.zeros((8, CZ), F32) for _ in range(2)]
            for j in range(4):
                y = b * 4 + j
                for t in range(T):
                    scale = dg[t, pl.ds(pl.multiple_of(y * 8, 8), 8), :]
                    for f, (center, total) in enumerate(change(p, k, t, y)):
                        sums[f] = sums[f] + scale * (total - RELAX * center)
            for f in range(2):
                rbuf[pl.ds(f * 128 + b, 8, stride=12), :] = sums[f]
            return carry

        lax.fori_loop(0, CY // 4, one, 0)

    def all_to_all(src, dst, send, recv, own):
        keep = pltpu.make_async_copy(src.at[me], dst.at[me], recv)
        keep.start()

        def one(i, carry):
            other, device = peer(i)
            pltpu.make_async_remote_copy(
                src.at[other], dst.at[me], send, recv, device_id=device, device_id_type=MESH
            ).start()
            return carry

        lax.fori_loop(1, n, one, 0)

    def finish(src, dst, send, recv):
        pltpu.make_async_copy(dst, dst, recv).wait()
        pltpu.make_async_copy(src.at[0:n - 1], src.at[0:n - 1], send).wait()

    def coarse(cycle):
        gbuf[...] = jnp.dot(p_out[...], rbuf[...].astype(BF16), preferred_element_type=F32)

        def pack(i, carry):
            rows = gbuf[pl.ds(pl.multiple_of(i * 8, 8), 8), :].astype(BF16)
            send_a[cycle, 2 * i] = rows[0:4]
            send_a[cycle, 2 * i + 1] = rows[4:8]
            return carry

        lax.fori_loop(0, n // 2, pack, 0, unroll=4)
        all_to_all(send_a.at[cycle], recv_a.at[cycle], a_s.at[cycle], a_r.at[cycle], me)
        if cycle == 0:
            mats_copy.wait()
        finish(send_a.at[cycle], recv_a.at[cycle], a_s.at[cycle], a_r.at[cycle])
        first_slot = lax.broadcasted_iota(jnp.int32, (4, CZ), 0) < 2

        def apply(i, carry):
            both = mats[pl.ds(2 * i, 2)].reshape(2 * CZ, CZ)
            product = lax.dot_general(recv_a[cycle, i], both, CONTRACT_LAST, preferred_element_type=F32)
            send_b[cycle, i] = jnp.where(first_slot, product[:, :CZ], product[:, CZ:])
            return carry

        lax.fori_loop(0, n, apply, 0, unroll=8)
        all_to_all(send_b.at[cycle], recv_b.at[cycle], b_s.at[cycle], b_r.at[cycle], me)
        finish(send_b.at[cycle], recv_b.at[cycle], b_s.at[cycle], b_r.at[cycle])

        def unpack(i, carry):
            gbuf[pl.ds(pl.multiple_of(i * 8, 8), 8), :] = jnp.concatenate(
                [recv_b[cycle, 2 * i], recv_b[cycle, 2 * i + 1]], axis=0
            )
            return carry

        lax.fori_loop(0, n // 2, unpack, 0, unroll=4)
        rows = gbuf[...]
        high = rows.astype(BF16)
        low = (rows - high.astype(F32)).astype(BF16)
        cbuf[...] = jnp.dot(p_in[...], high, preferred_element_type=F32) + jnp.dot(
            p_in[...], low, preferred_element_type=F32
        )

    def correct(p, k):
        q = 1 - p

        def one(b, carry):
            for f in range(2):
                extra = cbuf[pl.ds(f * 128 + b, 8, stride=12), :]
                for j in range(4):
                    y = b * 4 + j
                    for t in range(T):
                        put(q, k, f, t, y, field_of(p, f)(t, y * 8 + 8) + extra)
            return carry

        lax.fori_loop(0, CY // 4, one, 0)

    def arrive(copies):
        for copy in copies:
            copy.wait()

    k, p = 0, 0
    moving = exchange(p, k)
    for cycle in range(CYCLES):
        for step in range(1 if cycle == 0 else 2):
            arrive(moving)
            sweep(p, k)
            k, p = k + 1, 1 - p
            moving = exchange(p, k)
        arrive(moving)
        residual(p, k)
        coarse(cycle)
        k = k + 1
        correct(p, k)
        p = 1 - p
        moving = exchange(p, k)
        for step in range(2):
            arrive(moving)
            sweep(p, k)
            k, p = k + 1, 1 - p
            moving = exchange(p, k)

    arrive(moving)
    for f in range(2):
        xs[p, f, :, 0:8] = xs[p, f, :, 0:8] * in_s
        xs[p, f, :, ROWS + 8:PAD] = xs[p, f, :, ROWS + 8:PAD] * in_n
        hx[k, 0, f] = hx[k, 0, f] * in_w
        hx[k, 1, f] = hx[k, 1, f] * in_e
    for side in range(2):
        hdx[side] = hdx[side] + hx[k, side, 0]

    def update(i, carry):
        row = pl.multiple_of(i * 8, 8)
        for t in range(T):
            hl[t, pl.ds(row, 8), :] = hl[t, pl.ds(row, 8), :] + xs[p, 0, t, pl.ds(row, 8), :]
        return carry

    lax.fori_loop(0, PAD // 8, update, 0)

    def gradient(y, carry):
        for t in range(T):
            h_c, h_all = beside(plain(hl), side_row(hdx, 0), side_row(hdx, 1), t, y, False)
            a_c, a_all = beside(field_of(p, 1), halo_row(k, 0, 1), halo_row(k, 1, 1), t, y, False)
            total = jnp.zeros((8, CZ), F32)
            for h_o, a_o in zip(h_all, a_all):
                total = total + (a_c - a_o) * (h_c - h_o)
            grad[pl.ds(pl.multiple_of(t * ROWS + y * 8, 8), 8), :] = total
        return carry

    lax.fori_loop(0, CY, gradient, 0)

    ones = jnp.ones((8, CZ), BF16)
    for block in range(T):
        cut = slice(block * ROWS, block * ROWS + ROWS)
        rows = grad[cut, :]
        high = rows.astype(BF16)
        low = (rows - high.astype(F32)).astype(BF16)
        column = lax.dot_general(ones, high, CONTRACT_LAST, preferred_element_type=F32)
        column = column + lax.dot_general(ones, low, CONTRACT_LAST, preferred_element_type=F32)
        column = column[0:1] * (-0.5 / CZ)
        high = column.astype(BF16).astype(F32)
        low = column - high
        mine = lax.broadcasted_iota(jnp.int32, (n, ROWS), 0).astype(F32) == zone_dev[:, cut]
        parts = jnp.zeros((n, ZDEV), F32)
        for value in (high, low):
            spread = jnp.where(mine, value, 0.0).astype(BF16)
            parts = parts + lax.dot_general(spread, zone_hot[:, cut], CONTRACT_LAST, preferred_element_type=F32)
        if block == 0:
            lz[...] = parts
        else:
            lz[...] += parts

    def pack_zones(i, carry):
        rows = lz[pl.ds(pl.multiple_of(i * 8, 8), 8), :]
        for j in range(8):
            send_z[8 * i + j] = rows[j:j + 1]
        return carry

    lax.fori_loop(0, n // 8, pack_zones, 0)
    all_to_all(send_z, recv_z, z_s, z_r, me)

    def natural(t, carry):
        for s in range(8):
            for block in range(CY // 8):
                onat[4 * s + t, block * 8:block * 8 + 8, :] = hl[t, pl.ds(8 + block * 64 + s, 8, stride=8), :]
        return carry

    lax.fori_loop(0, T, natural, 0)
    out_copy = pltpu.make_async_copy(onat, out_head, out_sem)
    out_copy.start()
    finish(send_z, recv_z, z_s, z_r)

    def add_zones(i, total):
        return total + recv_z[i]

    out_zone[...] = lax.fori_loop(0, n, add_zones, jnp.zeros((1, ZDEV), F32), unroll=8)
    out_copy.wait()


def on_device(
    head, conductivity, storage, recharge, misfit, reservoir_cell, pumping, observed, tile_owner, tile_inverse, zone_of_column
):
    nx, ny = lax.axis_size("gx"), lax.axis_size("gy")
    n = nx * ny
    zone = jnp.transpose(zone_of_column.reshape(8, T, CY), (1, 2, 0)).reshape(1, CX * CY)
    anywhere, vmem = pl.BlockSpec(memory_space=pl.ANY), pl.BlockSpec(memory_space=pltpu.VMEM)
    dma = pltpu.SemaphoreType.DMA
    new_head, zones = pl.pallas_call(
        functools.partial(kernel, nx, ny),
        out_shape=(
            jax.ShapeDtypeStruct((CX, CY, CZ), F32),
            jax.ShapeDtypeStruct((1, ZDEV), F32),
        ),
        in_specs=[anywhere] * 5 + [vmem] * 4 + [anywhere, vmem],
        out_specs=(anywhere, vmem),
        scratch_shapes=[
            pltpu.VMEM((5, CX, CY, CZ), F32),
            pltpu.VMEM((2 * n, CZ, CZ), BF16),
            pltpu.VMEM((T, PAD, CZ), F32),
            pltpu.VMEM((T, PAD, CZ), F32),
            pltpu.VMEM((2, CY, CZ), F32),
            pltpu.VMEM((2, CY, CZ), F32),
            pltpu.VMEM((6, T, ROWS, CZ), F32),
            pltpu.VMEM((T, ROWS, CZ), F32),
            pltpu.VMEM((2, T, ROWS, CZ), F32),
            pltpu.VMEM((2, 2, T, PAD, CZ), F32),
            pltpu.VMEM((EXCHANGES, 2, 2, CY, CZ), F32),
            pltpu.VMEM((EXCHANGES, 2, 2, CY, CZ), F32),
            pltpu.VMEM((CX * CY, CZ), F32),
            pltpu.VMEM((CX, CY, CZ), F32),
            pltpu.VMEM((1, 128), F32),
            pltpu.VMEM((4 * n, 256), BF16),
            pltpu.VMEM((256, 4 * n), BF16),
            pltpu.VMEM((ZDEV, CX * CY), BF16),
            pltpu.VMEM((256, CZ), F32),
            pltpu.VMEM((4 * n, CZ), F32),
            pltpu.VMEM((256, CZ), F32),
            pltpu.VMEM((CYCLES, n, 4, CZ), BF16),
            pltpu.VMEM((CYCLES, n, 4, CZ), BF16),
            pltpu.VMEM((CYCLES, n, 4, CZ), F32),
            pltpu.VMEM((CYCLES, n, 4, CZ), F32),
            pltpu.VMEM((n, ZDEV), F32),
            pltpu.VMEM((n, 1, ZDEV), F32),
            pltpu.VMEM((n, 1, ZDEV), F32),
            dma((5,)), dma, dma, dma((8,)), dma((8,)), dma((EXCHANGES, 4)), dma((EXCHANGES, 4)),
            dma((CYCLES,)), dma((CYCLES,)), dma((CYCLES,)), dma((CYCLES,)), dma, dma,
        ],
        compiler_params=pltpu.CompilerParams(
            collective_id=0, has_side_effects=True, vmem_limit_bytes=60 * 1024 * 1024
        ),
        name="newton",
    )(
        head, conductivity, storage, recharge, misfit, reservoir_cell.reshape(1, -1), pumping.reshape(1, -1),
        observed.reshape(1, -1), tile_owner.reshape(1, -1), tile_inverse, zone,
    )
    return new_head, zones.reshape(ZDEV)


def solution(mesh):
    block, flat = P("gx", "gy", None), P(("gx", "gy"))
    placed = (block,) * 5 + (flat,) * 3 + (P(("gx", "gy"), None), P(("gx", "gy"), None, None), P("gx", "gy"))
    return jax.shard_map(
        on_device, mesh=mesh, in_specs=placed, out_specs=(block, flat), check_vma=False
    )
```

time: 500 us -> 160 us (0.32)
  waiting for transfers between devices: 185 us -> 0 us
  Pallas kernels: 0 us -> 154 us
  starting transfers between devices: 142 us -> 0 us
  blocking collectives: 69.6 us -> 0 us
  other arithmetic: 48.8 us -> 1.26 us
  local copies, waits for them, and re-layouts: 21 us -> 3.57 us
  matrix products: 16.3 us -> 0 us
  between operations: 15.4 us -> 0.65 us
    pallas_call x0 -> x1, Pallas kernels: none -> 154 us  [on_device(): pl.pallas_call(functools.partial(kernel, nx, ny), out_shape=(jax.ShapeDty...]
    unnamed x2 -> x0, waiting for transfers between devices: 149 us -> none
    ppermute x44 -> x0, starting transfers between devices: 137 us -> none  [the longest x22 95.5 us: extended(): before = lax.ppermute(last, axis, up)]
    all_to_all x3 -> x0, blocking collectives: 69.6 us -> none  [the longest x2 54.4 us: on_device(): lax.all_to_all(outgoing.reshape(devices, capacity, 2, layers), ('gx', 'gy...]
    ppermute x44 -> x0, waiting for transfers between devices: 25.6 us -> none  [the longest x22 14.9 us: extended(): before = lax.ppermute(last, axis, up)]
    add x11 -> x0, other arithmetic: 19.1 us -> none  [the longest x7 18.3 us: smooth(): state = state + relax * (rhs - apply_operator(near, storage, conds)) / total]
    dot_general x2 -> x0, matrix products: 16.3 us -> none  [on_device(): jnp.einsum('smij,smfj->smfi', tile_inverse.reshape(devices, capacity, lay...]
    scatter-add x3 -> x0, other arithmetic: 11.9 us -> none  [the longest x1 9.24 us: on_device(): jax.ops.segment_sum(column.reshape(-1), zone_of_column.reshape(-1), num_s...]
  transfers between devices with their start and end apart: 46 -> 0, of which waited for: 24 -> 0; matrix products, arithmetic and copies ran while one was open for 2% -> 0% of each run, Pallas kernels for 0% -> 0%
where the time goes in v1:
time: 160 us; the launch traced here: 159 us
  Pallas kernels  154 us (96%)
  local copies, waits for them, and re-layouts  3.57 us (2%)
    pallas_call x1, Pallas kernels, on_device(): pl.pallas_call(functools.partial(kernel, nx, ny), out_shape=(jax.ShapeDty...  154 us

profile of v1, /device:TPU:1, one launch (start us, length us, event | category | flops | bytes accessed | tf_op | source)
XLA Modules:
  0.0 159.5 jit_solution(7739955271352762701)
XLA Ops:
  0.6 0.8 copy.14
  1.4 0.7 reshape.30.zone
  2.1 154.0 %newton.1 = (f32[32,48,128]{2,1,0:T(8,128)}, f32[1,384]{1,0:T(1,128)}) custom-call(f32[32,48,128]{2,1,0:T(8,128)} %head.1, f32[32,48,128]{2,1,0:T(8,128)} %cond.1, f32[32,48,128]{2,1,0:T(8,128)} %stor.1, f32[32,48,128]{2,1,0:T(8,128)} %rech.1, f32[32,48,128]{2,1,0:T(8,128)} %misf.1, s32[1,16]{1,0:T(1,128)} %bitcast.8, f32[1,16]{1,0:T(1,128)} %bitcast.9, ...), custom_call_target="tpu_custom_call" | custom-call | tf_op jit(solution)/shard_map/newton/pallas_call | solution.py:456
  156.2 1.3 reduce
  157.4 2.1 %copy.16 = f32[32,48,128]{2,1,0:T(8,128)} copy(f32[32,48,128]{2,1,0:T(8,128)} %get-tuple-element.8) | data formatting | bytes 1572864

commit v2 on v1

--- a/solution.py
+++ b/solution.py
@@ -25,11 +25,12 @@
     nx, ny,
     head, cond, stor, rech, misf, cells, pump, obs, owner, mats_in, zone,
     out_head, out_zone,
-    nat, mats, kl, hl, kx, hdx, ecf, dg, rs, xs, sx, hx, grad, onat, owner_row, p_out, p_in, zone_hot,
+    nat, mats, kl, hl, kx, hdx, ecf, dg, rs, xa, xb, sx, hx, edge_x, face_x, edge_y, face_y, prods, grad, onat, owner_row, p_out, p_in, zone_hot,
     rbuf, gbuf, cbuf, send_a, recv_a, send_b, recv_b, lz, send_z, recv_z,
     load_sem, mats_sem, out_sem, init_s, init_r, halo_s, halo_r, a_s, a_r, b_s, b_r, z_s, z_r,
 ):
     n = nx * ny
+    xs = (xa, xb)
     me_x, me_y = lax.axis_index("gx"), lax.axis_index("gy")
     me = me_x * ny + me_y
     east, west = (lax.rem(me_x + 1, nx), me_y), (lax.rem(me_x + nx - 1, nx), me_y)
@@ -179,7 +180,7 @@
         return lambda t, row: ref[t, pl.ds(pl.multiple_of(row, 8), 8), :]
 
     def field_of(p, f):
-        return lambda t, row: xs[p, f, t, pl.ds(pl.multiple_of(row, 8), 8), :]
+        return lambda t, row: xs[p][f, t, pl.ds(pl.multiple_of(row, 8), 8), :]
 
     def side_row(ref, side):
         return lambda y: ref[side, pl.ds(y, 1), :]
@@ -188,7 +189,7 @@
         return lambda y: hx[k, side, f, pl.ds(y, 1), :]
 
     def put(p, k, f, t, y, value):
-        xs[p, f, t, pl.ds(pl.multiple_of(y * 8 + 8, 8), 8), :] = value
+        xs[p][f, t, pl.ds(pl.multiple_of(y * 8 + 8, 8), 8), :] = value
         if t == 0:
             sx[k, 0, f, pl.ds(y, 1), :] = value[0:1]
         if t == T - 1:
@@ -198,8 +199,8 @@
         return [
             remote(sx.at[k, 1], hx.at[k, 0], halo_s.at[k, 0], halo_r.at[k, 0], east),
             remote(sx.at[k, 0], hx.at[k, 1], halo_s.at[k, 1], halo_r.at[k, 1], west),
-            remote(xs.at[p, :, :, ROWS:ROWS + 8], xs.at[p, :, :, 0:8], halo_s.at[k, 2], halo_r.at[k, 2], north),
-            remote(xs.at[p, :, :, 8:16], xs.at[p, :, :, ROWS + 8:PAD], halo_s.at[k, 3], halo_r.at[k, 3], south),
+            remote(xs[p].at[:, :, ROWS:ROWS + 8], xs[p].at[:, :, 0:8], halo_s.at[k, 2], halo_r.at[k, 2], north),
+            remote(xs[p].at[:, :, 8:16], xs[p].at[:, :, ROWS + 8:PAD], halo_s.at[k, 3], halo_r.at[k, 3], south),
         ]
 
     def prepare(y, carry):
@@ -230,64 +231,135 @@
                 put(0, 0, f, t, y, rhs)
         return carry
 
-    lax.fori_loop(0, CY, prepare, 0)
-    ecf[2, :, 0:8] = ecf[2, :, 0:8] * in_s
-    ecf[3, :, ROWS - 8:ROWS] = ecf[3, :, ROWS - 8:ROWS] * in_n
-
-    def change(p, k, t, y):
+    lax.fori_loop(0, CY, prepare, 0, unroll=2)
+
+    def split_edges():
+        edge_y[0] = ecf[2, :, 0:8] * in_s
+        edge_y[1] = ecf[3, :, ROWS - 8:ROWS] * in_n
+        face_y[0] = edge_y[0] * dg[:, 0:8]
+        face_y[1] = edge_y[1] * dg[:, ROWS - 8:ROWS]
+        for block in range(CY // 8):
+            cut = slice(block * 8, block * 8 + 8)
+            for side, t, s in ((0, 0, 0), (1, T - 1, 7)):
+                rows = pl.ds(block * 64 + s, 8, stride=8)
+                edge_x[side, cut] = ecf[side, t, rows, :]
+                face_x[side, cut] = edge_x[side, cut] * dg[t, rows, :]
+
+        def clear(y, carry):
+            rows = pl.ds(pl.multiple_of(y * 8, 8), 8)
+            ecf[0, 0, rows, :] = jnp.where(low_s, 0.0, ecf[0, 0, rows, :])
+            ecf[1, T - 1, rows, :] = jnp.where(high_s, 0.0, ecf[1, T - 1, rows, :])
+            return carry
+
+        lax.fori_loop(0, CY, clear, 0, unroll=8)
+
+    def change(p, t, y, south=True, north=True):
         row = pl.multiple_of(y * 8, 8)
         factors = [ecf[j, t, pl.ds(row, 8), :] for j in range(6)]
         result = []
         for f in range(2):
-            center, others = beside(field_of(p, f), halo_row(k, 0, f), halo_row(k, 1, f), t, y, True)
+            tile = field_of(p, f)
+            center = tile(t, row + 8)
+            wst = tile(t - 1, row + 8) if t else pltpu.roll(tile(T - 1, row + 8), 1, 0)
+            est = tile(t + 1, row + 8) if t < T - 1 else pltpu.roll(tile(0, row + 8), 7, 0)
+            others = [wst, est, tile(t, row) if south else None, tile(t, row + 16) if north else None]
+            others += [pltpu.roll(center, 1, 1), pltpu.roll(center, CZ - 1, 1)]
             total = rs[f, t, pl.ds(row, 8), :]
             for factor, other in zip(factors, others):
-                total = total + factor * other
+                if other is not None:
+                    total = total + factor * other
             result.append((center, total))
         return result
 
-    def sweep(p, k):
+    def sweep(p):
         q = 1 - p
 
-        def one(y, carry):
+        def row_of(y, **sides):
             for t in range(T):
-                for f, (center, total) in enumerate(change(p, k, t, y)):
-                    put(q, k + 1, f, t, y, (1.0 - RELAX) * center + total)
-            return carry
-
-        lax.fori_loop(0, CY, one, 0)
-
-    def residual(p, k):
-        def one(b, carry):
+                for f, (center, total) in enumerate(change(p, t, y, **sides)):
+                    xs[q][f, t, pl.ds(pl.multiple_of(y * 8 + 8, 8), 8), :] = (1.0 - RELAX) * center + total
+
+        def one(i, carry):
+            row_of(2 * i + 1)
+            row_of(2 * i + 2)
+            return carry
+
+        row_of(0, south=False)
+        lax.fori_loop(0, CY // 2 - 1, one, 0)
+        row_of(CY - 1, north=False)
+
+    def sweep_edges(p, k):
+        q = 1 - p
+        for f in range(2):
+            for t in range(T):
+                xs[q][f, t, 8:16] += edge_y[0, t] * xs[p][f, t, 0:8]
+                xs[q][f, t, ROWS:ROWS + 8] += edge_y[1, t] * xs[p][f, t, ROWS + 8:PAD]
+            for block in range(CY // 8):
+                cut = slice(block * 8, block * 8 + 8)
+                for side, t, s in ((0, 0, 0), (1, T - 1, 7)):
+                    rows = pl.ds(8 + block * 64 + s, 8, stride=8)
+                    value = xs[q][f, t, rows, :] + edge_x[side, cut] * hx[k, side, f, cut]
+                    xs[q][f, t, rows, :] = value
+                    sx[k + 1, side, f, cut] = value
+
+    def residual(p):
+        def block_of(b, first=False, last=False):
             sums = [jnp.zeros((8, CZ), F32) for _ in range(2)]
             for j in range(4):
                 y = b * 4 + j
                 for t in range(T):
                     scale = dg[t, pl.ds(pl.multiple_of(y * 8, 8), 8), :]
-                    for f, (center, total) in enumerate(change(p, k, t, y)):
+                    both = change(p, t, y, south=not (first and j == 0), north=not (last and j == 3))
+                    for f, (center, total) in enumerate(both):
                         sums[f] = sums[f] + scale * (total - RELAX * center)
             for f in range(2):
                 rbuf[pl.ds(f * 128 + b, 8, stride=12), :] = sums[f]
-            return carry
-
-        lax.fori_loop(0, CY // 4, one, 0)
-
-    def all_to_all(src, dst, send, recv, own):
-        keep = pltpu.make_async_copy(src.at[me], dst.at[me], recv)
-        keep.start()
-
+
+        def one(b, carry):
+            block_of(b)
+            return carry
+
+        block_of(0, first=True)
+        lax.fori_loop(1, CY // 4 - 1, one, 0)
+        block_of(CY // 4 - 1, last=True)
+
+    def residual_edges(p, k):
+        for f in range(2):
+            for side, b in ((0, 0), (1, CY // 4 - 1)):
+                pad = slice(0, 8) if side == 0 else slice(ROWS + 8, PAD)
+                rows = pl.ds(f * 128 + b, 8, stride=12)
+                rbuf[rows, :] += sum(face_y[side, t] * xs[p][f, t, pad] for t in range(T))
+        for f in range(2):
+            for side in range(2):
+                prods[f, side] = face_x[side] * hx[k, side, f]
+        for f in range(2):
+            for side, start in ((0, f * 128), (1, f * 128 + 84)):
+                rbuf[start:start + 12, :] += sum(prods[f, side, pl.ds(j, 12, stride=4), :] for j in range(4))
+
+    def send_to(i, src, dst, send, recv):
+        other, device = peer(i)
+        pltpu.make_async_remote_copy(
+            src.at[other], dst.at[me], send, recv, device_id=device, device_id_type=MESH
+        ).start()
+
+    def send_all(src, dst, send, recv):
         def one(i, carry):
-            other, device = peer(i)
-            pltpu.make_async_remote_copy(
-                src.at[other], dst.at[me], send, recv, device_id=device, device_id_type=MESH
-            ).start()
-            return carry
-
-        lax.fori_loop(1, n, one, 0)
-
-    def finish(src, dst, send, recv):
+            for j in range(7):
+                send_to(7 * i + j + 1, src, dst, send, recv)
+            return carry
+
+        lax.fori_loop(0, (n - 2) // 7, one, 0)
+        for i in range((n - 2) // 7 * 7 + 1, n):
+            send_to(i, src, dst, send, recv)
+
+    def keep(src, dst, recv):
+        pltpu.make_async_copy(src.at[me], dst.at[me], recv).start()
+
+    def sent(src, send):
+        pltpu.make_async_copy(src.at[0:n - 1], src.at[0:n - 1], send).wait()
+
+    def received(dst, recv):
         pltpu.make_async_copy(dst, dst, recv).wait()
-        pltpu.make_async_copy(src.at[0:n - 1], src.at[0:n - 1], send).wait()
 
     def coarse(cycle):
         gbuf[...] = jnp.dot(p_out[...], rbuf[...].astype(BF16), preferred_element_type=F32)
@@ -299,21 +371,47 @@
             return carry
 
         lax.fori_loop(0, n // 2, pack, 0, unroll=4)
-        all_to_all(send_a.at[cycle], recv_a.at[cycle], a_s.at[cycle], a_r.at[cycle], me)
+        keep(send_a.at[cycle], recv_a.at[cycle], a_r.at[me])
+        send_all(send_a.at[cycle], recv_a.at[cycle], a_s, a_r.at[me])
         if cycle == 0:
             mats_copy.wait()
-        finish(send_a.at[cycle], recv_a.at[cycle], a_s.at[cycle], a_r.at[cycle])
         first_slot = lax.broadcasted_iota(jnp.int32, (4, CZ), 0) < 2
 
-        def apply(i, carry):
-            both = mats[pl.ds(2 * i, 2)].reshape(2 * CZ, CZ)
-            product = lax.dot_general(recv_a[cycle, i], both, CONTRACT_LAST, preferred_element_type=F32)
-            send_b[cycle, i] = jnp.where(first_slot, product[:, :CZ], product[:, CZ:])
-            return carry
-
-        lax.fori_loop(0, n, apply, 0, unroll=8)
-        all_to_all(send_b.at[cycle], recv_b.at[cycle], b_s.at[cycle], b_r.at[cycle], me)
-        finish(send_b.at[cycle], recv_b.at[cycle], b_s.at[cycle], b_r.at[cycle])
+        def answer(steps):
+            sources = [lax.rem(me - i + n, n) for i in steps]
+            for source in sources:
+                rows = recv_a.at[cycle, source]
+                pltpu.make_async_copy(rows, rows, a_r.at[source]).wait()
+            for source in sources:
+                both = mats[pl.ds(2 * source, 2)].reshape(2 * CZ, CZ)
+                product = lax.dot_general(recv_a[cycle, source], both, CONTRACT_LAST, preferred_element_type=F32)
+                send_b[cycle, source] = jnp.where(first_slot, product[:, :CZ], product[:, CZ:])
+
+        def reply(i):
+            source = lax.rem(me - i + n, n)
+            device = (lax.div(source, ny), lax.rem(source, ny))
+            pltpu.make_async_remote_copy(
+                send_b.at[cycle, source], recv_b.at[cycle, me], b_s, b_r, device_id=device, device_id_type=MESH
+            ).start()
+
+        answer([0])
+        keep(send_b.at[cycle], recv_b.at[cycle], b_r)
+
+        def some(i, carry):
+            steps = [7 * i + j + 1 for j in range(7)]
+            answer(steps)
+            for step in steps:
+                reply(step)
+            return carry
+
+        lax.fori_loop(0, (n - 2) // 7, some, 0)
+        rest = list(range((n - 2) // 7 * 7 + 1, n))
+        answer(rest)
+        for step in rest:
+            reply(step)
+        sent(send_a.at[cycle], a_s)
+        received(recv_b.at[cycle], b_r)
+        sent(send_b.at[cycle], b_s)
 
         def unpack(i, carry):
             gbuf[pl.ds(pl.multiple_of(i * 8, 8), 8), :] = jnp.concatenate(
@@ -329,19 +427,42 @@
             p_in[...], low, preferred_element_type=F32
         )
 
-    def correct(p, k):
+    def correct_edges(p, k):
         q = 1 - p
-
-        def one(b, carry):
+        for f in range(2):
+            for y, b in ((0, 0), (CY - 1, CY // 4 - 1)):
+                extra = cbuf[pl.ds(f * 128 + b, 8, stride=12), :]
+                for t in range(T):
+                    xs[q][f, t, y * 8 + 8:y * 8 + 16] = xs[p][f, t, y * 8 + 8:y * 8 + 16] + extra
+            for block in range(CY // 8):
+                for side, t, s in ((0, 0, 0), (1, T - 1, 7)):
+                    at = f * 128 + s * 12 + block * 2
+                    extra = jnp.where(
+                        sub8 < 4,
+                        jnp.broadcast_to(cbuf[at:at + 1], (8, CZ)),
+                        jnp.broadcast_to(cbuf[at + 1:at + 2], (8, CZ)),
+                    )
+                    rows = pl.ds(8 + block * 64 + s, 8, stride=8)
+                    sx[k, side, f, block * 8:block * 8 + 8] = xs[p][f, t, rows, :] + extra
+
+    def correct(p):
+        q = 1 - p
+
+        def block_of(b, js):
             for f in range(2):
                 extra = cbuf[pl.ds(f * 128 + b, 8, stride=12), :]
-                for j in range(4):
-                    y = b * 4 + j
+                for j in js:
                     for t in range(T):
-                        put(q, k, f, t, y, field_of(p, f)(t, y * 8 + 8) + extra)
-            return carry
-
-        lax.fori_loop(0, CY // 4, one, 0)
+                        rows = pl.ds(pl.multiple_of((b * 4 + j) * 8 + 8, 8), 8)
+                        xs[q][f, t, rows, :] = xs[p][f, t, rows, :] + extra
+
+        def one(b, carry):
+            block_of(b, range(4))
+            return carry
+
+        block_of(0, (1, 2, 3))
+        lax.fori_loop(1, CY // 4 - 1, one, 0)
+        block_of(CY // 4 - 1, (0, 1, 2))
 
     def arrive(copies):
         for copy in copies:
@@ -349,29 +470,34 @@
 
     k, p = 0, 0
     moving = exchange(p, k)
+    split_edges()
     for cycle in range(CYCLES):
         for step in range(1 if cycle == 0 else 2):
+            sweep(p)
             arrive(moving)
-            sweep(p, k)
+            sweep_edges(p, k)
             k, p = k + 1, 1 - p
             moving = exchange(p, k)
+        residual(p)
         arrive(moving)
-        residual(p, k)
+        residual_edges(p, k)
         coarse(cycle)
         k = k + 1
-        correct(p, k)
+        correct_edges(p, k)
+        moving = exchange(1 - p, k)
+        correct(p)
         p = 1 - p
-        moving = exchange(p, k)
         for step in range(2):
+            sweep(p)
             arrive(moving)
-            sweep(p, k)
+            sweep_edges(p, k)
             k, p = k + 1, 1 - p
             moving = exchange(p, k)
 
     arrive(moving)
     for f in range(2):
-        xs[p, f, :, 0:8] = xs[p, f, :, 0:8] * in_s
-        xs[p, f, :, ROWS + 8:PAD] = xs[p, f, :, ROWS + 8:PAD] * in_n
+        xs[p][f, :, 0:8] = xs[p][f, :, 0:8] * in_s
+        xs[p][f, :, ROWS + 8:PAD] = xs[p][f, :, ROWS + 8:PAD] * in_n
         hx[k, 0, f] = hx[k, 0, f] * in_w
         hx[k, 1, f] = hx[k, 1, f] * in_e
     for side in range(2):
@@ -380,7 +506,7 @@
     def update(i, carry):
         row = pl.multiple_of(i * 8, 8)
         for t in range(T):
-            hl[t, pl.ds(row, 8), :] = hl[t, pl.ds(row, 8), :] + xs[p, 0, t, pl.ds(row, 8), :]
+            hl[t, pl.ds(row, 8), :] = hl[t, pl.ds(row, 8), :] + xs[p][0, t, pl.ds(row, 8), :]
         return carry
 
     lax.fori_loop(0, PAD // 8, update, 0)
@@ -395,7 +521,7 @@
             grad[pl.ds(pl.multiple_of(t * ROWS + y * 8, 8), 8), :] = total
         return carry
 
-    lax.fori_loop(0, CY, gradient, 0)
+    lax.fori_loop(0, CY, gradient, 0, unroll=2)
 
     ones = jnp.ones((8, CZ), BF16)
     for block in range(T):
@@ -425,7 +551,8 @@
         return carry
 
     lax.fori_loop(0, n // 8, pack_zones, 0)
-    all_to_all(send_z, recv_z, z_s, z_r, me)
+    keep(send_z, recv_z, z_r)
+    send_all(send_z, recv_z, z_s, z_r)
 
     def natural(t, carry):
         for s in range(8):
@@ -436,7 +563,8 @@
     lax.fori_loop(0, T, natural, 0)
     out_copy = pltpu.make_async_copy(onat, out_head, out_sem)
     out_copy.start()
-    finish(send_z, recv_z, z_s, z_r)
+    received(recv_z, z_r)
+    sent(send_z, z_s)
 
     def add_zones(i, total):
         return total + recv_z[i]
@@ -471,9 +599,15 @@
             pltpu.VMEM((6, T, ROWS, CZ), F32),
             pltpu.VMEM((T, ROWS, CZ), F32),
             pltpu.VMEM((2, T, ROWS, CZ), F32),
-            pltpu.VMEM((2, 2, T, PAD, CZ), F32),
+            pltpu.VMEM((2, T, PAD, CZ), F32),
+            pltpu.VMEM((2, T, PAD, CZ), F32),
             pltpu.VMEM((EXCHANGES, 2, 2, CY, CZ), F32),
             pltpu.VMEM((EXCHANGES, 2, 2, CY, CZ), F32),
+            pltpu.VMEM((2, CY, CZ), F32),
+            pltpu.VMEM((2, CY, CZ), F32),
+            pltpu.VMEM((2, T, 8, CZ), F32),
+            pltpu.VMEM((2, T, 8, CZ), F32),
+            pltpu.VMEM((2, 2, CY, CZ), F32),
             pltpu.VMEM((CX * CY, CZ), F32),
             pltpu.VMEM((CX, CY, CZ), F32),
             pltpu.VMEM((1, 128), F32),
@@ -491,7 +625,7 @@
             pltpu.VMEM((n, 1, ZDEV), F32),
             pltpu.VMEM((n, 1, ZDEV), F32),
             dma((5,)), dma, dma, dma((8,)), dma((8,)), dma((EXCHANGES, 4)), dma((EXCHANGES, 4)),
-            dma((CYCLES,)), dma((CYCLES,)), dma((CYCLES,)), dma((CYCLES,)), dma, dma,
+            dma, dma((n,)), dma, dma, dma, dma,
         ],
         compiler_params=pltpu.CompilerParams(
             collective_id=0, has_side_effects=True, vmem_limit_bytes=60 * 1024 * 1024

time: 160 us -> 115 us (0.72)
  Pallas kernels: 154 us -> 109 us
    pallas_call x1, Pallas kernels: 154 us -> 109 us  [on_device(): pl.pallas_call(functools.partial(kernel, nx, ny), out_shape=(jax.ShapeDty...]
where the time goes in v2:
time: 115 us; the launch traced here: 114 us
  Pallas kernels  109 us (95%)
  local copies, waits for them, and re-layouts  3.57 us (3%)
  other arithmetic  1.26 us (1%)
    pallas_call x1, Pallas kernels, on_device(): pl.pallas_call(functools.partial(kernel, nx, ny), out_shape=(jax.ShapeDty...  109 us

profile of v2, /device:TPU:1, one launch (start us, length us, event | category | flops | bytes accessed | tf_op | source)
XLA Modules:
  0.0 114.3 jit_solution(15890351171738671148)
XLA Ops:
  0.6 0.8 copy.14
  1.4 0.7 reshape.30.zone
  2.1 108.8 %newton.1 = (f32[32,48,128]{2,1,0:T(8,128)}, f32[1,384]{1,0:T(1,128)}) custom-call(f32[32,48,128]{2,1,0:T(8,128)} %head.1, f32[32,48,128]{2,1,0:T(8,128)} %cond.1, f32[32,48,128]{2,1,0:T(8,128)} %stor.1, f32[32,48,128]{2,1,0:T(8,128)} %rech.1, f32[32,48,128]{2,1,0:T(8,128)} %misf.1, s32[1,16]{1,0:T(1,128)} %bitcast.8, f32[1,16]{1,0:T(1,128)} %bitcast.9, ...), custom_call_target="tpu_custom_call" | custom-call | tf_op jit(solution)/shard_map/newton/pallas_call | solution.py:584
  111.0 1.3 %reduce = f32[384]{0:T(512)} reduce(f32[1,384]{1,0:T(1,128)} %get-tuple-element.5, f32[]{:T(128)} %constant.4), dimensions={0}, to_apply=%get-tuple-element.5.reduce_sub_computation | reduce | bytes 3076 | tf_op jit(solution)/shard_map/newton/pallas_call | solution.py:584
  112.3 2.1 %copy.16 = f32[32,48,128]{2,1,0:T(8,128)} copy(f32[32,48,128]{2,1,0:T(8,128)} %get-tuple-element.8) | data formatting | bytes 1572864
